TPU v7x, 32 devices: a whole 2x2x4 slice. The times are simulated.
32 devices in a mesh: grp: 2 (over y), epoch: 4 (over x, core), asset: 4 (over z).
Axes of the slice: x: 2, y: 2, z: 4, core: 2. Of those that a mesh axis runs over, the one named last changes fastest.
Arguments:
- signals: bfloat16 [8, 1024, 256], P(('grp', 'epoch'), 'asset'), parts along dimension 0, may hold values from -6 to 6
- targets: bfloat16 [8, 1024, 256], P(('grp', 'epoch'), 'asset'), parts along dimension 0, may hold values from -6 to 6
- row_counts: int32 [8, 4], P(('grp', 'epoch'), 'asset'), parts along dimension 0, may hold values from 32 to 256, as said below
- feature_weights: bfloat16 [256, 2048], replicated, may hold values from -0.375 to 0.375
- phases: float32 [2048], replicated, may hold values from -3.140625 to 3.140625
- spread_ids: int32 [2048], replicated, may hold values from 0 to 3
Outputs:
- coefficients: float32 [8, 2048, 256], P(('grp', 'epoch'), 'asset'), parts along dimension 0
There are 2 independent parts, one for each index of `grp`. A program takes and returns all parts, laid end to end along the dimension named above; an argument that names none is the same for every part. Nothing has to cross between parts.
Inputs may be any that keep to these rules, and one draw needn't show every extreme that they name: `row_counts`: each count is at least 32, and in every epoch some asset group has exactly 256 live rows.
All inputs are finite; a program needn't handle non-finite values.
Results may differ from a plain program's by a relative error of at most 0.0003.
Values may be sent and summed in bfloat16 or wider, within the bound.
No kernel may reach another device: no remote copies, remote signals or barrier semaphores. Data moves between devices by JAX's collectives and lax.ppermute only.
A program may use at most 64 MiB of HBM per device.

v0:
```python
import jax
import jax.numpy as jnp
from jax import lax
from jax.sharding import PartitionSpec as P

ITERS = 3
ridge_penalty = 0.05
epsilon = 1e-06


def prefix(part, axis, combine, identity):
    place = lax.axis_index(axis)
    gathered = jax.tree.map(lambda a: lax.all_gather(a, axis), part)
    state = jax.tree.map(lambda a, e: jnp.zeros_like(a) + jnp.asarray(e, a.dtype), part, identity)

    def one(hop, state):
        return combine(
            state, jax.tree.map(lambda a: lax.dynamic_index_in_dim(a, hop, 0, False), gathered)
        )

    return lax.fori_loop(0, place, one, state)


def feature_scale(spread_ids):
    return (
        0.5
        * (
            1.0
            + jnp.where(spread_ids >= 1, 1.0, 0.0)
            + jnp.where(spread_ids >= 2, 2.0, 0.0)
            + jnp.where(spread_ids >= 3, 4.0, 0.0)
        )
    ).astype(jnp.float32)


def make_features(inputs, feature_weights, phases, spread_ids):
    projected = jnp.dot(inputs, feature_weights, preferred_element_type=jnp.float32)
    return jnp.sin(projected * feature_scale(spread_ids) + phases)


def add_pair(earlier, later):
    return (earlier[0] + later[0], earlier[1] + later[1])


def on_device(signals, targets, row_counts, feature_weights, phases, spread_ids):
    rows = signals.shape[1]
    width = feature_weights.shape[1]
    tgt_width = targets.shape[2]
    groups = lax.axis_size("asset")
    block_size = width // groups
    entries = width * tgt_width
    own_rows = row_counts[0, 0]
    all_counts = lax.all_gather(row_counts[0], "asset", axis=0, tiled=True)
    row_sum = jnp.sum(all_counts).astype(jnp.float32)
    inputs = signals[0]
    returns = targets[0]
    features = make_features(inputs, feature_weights, phases, spread_ids)
    live_mask = (jnp.arange(rows) < own_rows)[:, None]
    features = jnp.where(live_mask, features, jnp.zeros_like(features))
    returns = jnp.where(live_mask, returns.astype(jnp.float32), jnp.zeros((), jnp.float32))
    combined = jnp.concatenate([features, returns], axis=1)
    contract_rows = (((0,), (0,)), ((), ()))
    gram_block = lax.psum_scatter(
        lax.dot_general(features, combined, contract_rows, precision=lax.Precision.HIGHEST),
        "asset",
        scatter_dimension=0,
        tiled=True,
    )
    earlier, earlier_rows = prefix(
        (gram_block, row_sum),
        "epoch",
        add_pair,
        (jnp.zeros_like(gram_block), jnp.zeros((), jnp.float32)),
    )
    cumulative = earlier + gram_block
    row_total = earlier_rows + row_sum
    first_row = lax.axis_index("asset") * block_size
    diagonal = jnp.arange(width)[None, :] == first_row + jnp.arange(block_size)[:, None]
    system = cumulative[:, :width] / row_total + ridge_penalty * jnp.where(
        diagonal, 1.0, 0.0
    ).astype(jnp.float32)
    residual = cumulative[:, width:] / row_total
    coef = jnp.zeros((block_size, tgt_width), jnp.float32)
    for iteration in range(ITERS):
        image = jnp.zeros((block_size, tgt_width), jnp.float32) + jnp.dot(
            system,
            lax.all_gather(residual, "asset", axis=0, tiled=True),
            precision=lax.Precision.HIGHEST,
        )
        res_norm, res_curve = lax.psum(
            (jnp.sum(residual * residual), jnp.sum(residual * image)), "asset"
        )
        step_size = res_norm / entries / (res_curve / entries + epsilon)
        coef = coef + step_size * residual
        residual = residual - step_size * image
    return (jnp.sqrt(row_total) * coef)[None]


def solution(mesh):
    placed = (
        P(("grp", "epoch"), "asset", None),
        P(("grp", "epoch"), "asset", None),
        P(("grp", "epoch"), "asset"),
        P(),
        P(),
        P(),
    )
    return jax.shard_map(
        on_device,
        mesh=mesh,
        in_specs=placed,
        out_specs=P(("grp", "epoch"), "asset", None),
        check_vma=False,
    )
```

profile of v0, /device:TPU:0, one launch (start us, length us, event | category | flops | bytes accessed | tf_op | source)
XLA Modules:
  0.0 710.5 jit_solution(8003672284095175270)
XLA Ops:
  7.3 0.7 add_multiply_fusion
  8.0 1.0 convert_select_fusion
  9.0 8.1 %fusion.3 = f32[256,2048]{1,0:T(8,128)S(1)} fusion(bf16[256,2048]{1,0:T(8,128)(2,1)S(1)} %copy-done, f32[2048]{0:T(1024)} %param.12, f32[2048]{0:T(1024)S(1)} %add_multiply_fusion, pred[256]{0:T(512)(128)(4,1)S(1)} %iota_compare_fusion.1, bf16[1,256,256]{2,1,0:T(8,128)(2,1)} %param.8), kind=kOutput, calls=%fused_computation.7 | convolution fusion | flops 270008320 | bytes 3293440 | tf_op jit(solution)/shard_map/dot_general | solution.py:37
  17.1 19.4 %fusion.4 = f32[2048,2304]{1,0:T(8,128)} fusion(f32[256,2048]{1,0:T(8,128)S(1)} %fusion.3, f32[256,256]{1,0:T(8,128)S(1)} %convert_select_fusion), kind=kOutput, calls=%fused_computation.8 | convolution fusion | flops 14496104448 | bytes 21233664 | tf_op jit(solution)/shard_map/dot_general | solution.py:64
  36.6 316.7 %reduce-scatter.2.cloned.1.call-done = f32[512,2304]{1,0:T(8,128)} async-done(((f32[2048,2304]{1,0:T(8,128)}), f32[512,2304]{1,0:T(8,128)}) %reduce-scatter.2.cloned.1.call-update) | async-done | bytes 4718608 | tf_op jit(solution)/shard_map/reduce_scatter | solution.py:63
  353.4 0.6 dynamic-slice
  354.0 0.6 bitcast_dynamic-update-slice_fusion
  354.6 9.3 %all-reduce = s32[4]{0:T(128)S(1)} all-reduce(s32[4]{0:T(128)S(1)} %bitcast_dynamic-update-slice_fusion), channel_id=3, replica_groups=mesh['grp'=2,'epoch'=4,'asset'=4] {'asset'}, use_global_device_ids=true, to_apply=%add | all-reduce | flops 4 | bytes 32
  363.9 0.6 reduce.1
  365.2 0.6 dynamic-slice.1
  365.8 0.8 dynamic-update-slice.1
  366.6 5.6 all-reduce.1
  372.2 103.7 %all-gather.13.cloned.1.call-done = f32[2048,2304]{1,0:T(8,128)} async-done(((f32[512,2304]{1,0:T(8,128)}), f32[2048,2304]{1,0:T(8,128)}) %all-gather.13.cloned.1.call-update) | async-done | bytes 18874384 | tf_op jit(solution)/shard_map/all_gather | solution.py:13
  475.9 2.5 broadcast_in_dim.58
  478.4 4.3 add.88
  482.8 2.1 copy-done.2
  484.9 0.8 slice_divide_fusion.1
  485.7 0.0 all-gather.9.cloned.1.call-start
  485.8 5.1 fusion
  490.9 64.1 %all-gather.7.cloned.1.call-done = f32[2048,256]{1,0:T(8,128)} async-done(((f32[512,256]{1,0:T(8,128)}), f32[2048,256]{1,0:T(8,128)}) %all-gather.7.cloned.1.call-update) | async-done | bytes 2097168 | tf_op jit(solution)/shard_map/all_gather | solution.py:87
  555.1 6.6 multiply_reduce_fusion.3
  561.7 10.4 %all-reduce.4 = (f32[]{:T(128)}, f32[]{:T(128)}) all-reduce(f32[]{:T(128)} %get-tuple-element.44, f32[]{:T(128)} %get-tuple-element.43), channel_id=1, replica_groups=mesh['grp'=2,'epoch'=4,'asset'=4] {'asset'}, use_global_device_ids=true, to_apply=%region_5.6 | all-reduce | flops 2 | bytes 16 | tf_op jit(solution)/shard_map/psum | solution.py:90
  573.4 1.9 multiply_subtract_fusion.1
  575.3 0.3 all-gather.11.cloned.1.call-start
  575.6 43.8 %all-gather.9.cloned.1.call-done = f32[2048,256]{1,0:T(8,128)} async-done(((f32[512,256]{1,0:T(8,128)}), f32[2048,256]{1,0:T(8,128)}) %all-gather.9.cloned.1.call-update) | async-done | bytes 2097168 | tf_op jit(solution)/shard_map/all_gather | solution.py:87
  619.4 6.9 multiply_reduce_fusion.1
  626.3 10.4 %all-reduce.3 = (f32[]{:T(128)}, f32[]{:T(128)}) all-reduce(f32[]{:T(128)} %get-tuple-element.42, f32[]{:T(128)} %get-tuple-element.41), channel_id=1, replica_groups=mesh['grp'=2,'epoch'=4,'asset'=4] {'asset'}, use_global_device_ids=true, to_apply=%region_9.10 | all-reduce | flops 2 | bytes 16 | tf_op jit(solution)/shard_map/psum | solution.py:90
  638.0 1.4 multiply_reduce_fusion
  639.5 44.0 %all-gather.11.cloned.1.call-done = f32[2048,256]{1,0:T(8,128)} async-done(((f32[512,256]{1,0:T(8,128)}), f32[2048,256]{1,0:T(8,128)}) %all-gather.11.cloned.1.call-update) | async-done | bytes 2097168 | tf_op jit(solution)/shard_map/all_gather | solution.py:87
  683.5 6.9 fusion.8
  690.4 10.4 %all-reduce.2 = (f32[]{:T(128)}, f32[]{:T(128)}) all-reduce(f32[]{:T(128)} %get-tuple-element.63, f32[]{:T(128)} %fusion.8), channel_id=1, replica_groups=mesh['grp'=2,'epoch'=4,'asset'=4] {'asset'}, use_global_device_ids=true, to_apply=%region_13.14 | all-reduce | flops 2 | bytes 16 | tf_op jit(solution)/shard_map/psum | solution.py:90
  702.0 2.0 multiply_bitcast_fusion
  (28 shorter events, 0.2 us)
Async XLA Ops:
  6.5 2.5 copy-start
  6.5 346.8 %reduce-scatter.2.cloned.1.call-start = ((), (), s32[]{:S(2)}) async-start(), calls=%async_computation.1 | async-start | bytes 23592960 | tf_op jit(solution)/shard_map/reduce_scatter | solution.py:63
  36.5 316.9 %copy-start.7 = (u32[32]{0:T(128)S(1)}, u32[32]{0:T(128)}, u32[]{:S(2)}) copy-start(u32[32]{0:T(128)} %constant.59) | copy-start | bytes 388
  36.6 328.6 %copy-start.6 = (u32[32]{0:T(128)S(1)}, u32[32]{0:T(128)}, u32[]{:S(2)}) copy-start(u32[32]{0:T(128)} %constant.64) | copy-start | bytes 388
  36.6 439.3 %all-gather.13.cloned.1.call-start = ((), (), s32[]{:S(2)}) async-start(), calls=%async_computation.5 | async-start | bytes 23592960 | tf_op jit(solution)/shard_map/all_gather | solution.py:13
  353.4 201.7 %all-gather.7.cloned.1.call-start = ((), (), s32[]{:S(2)}) async-start(), calls=%async_computation.2 | async-start | bytes 2621440 | tf_op jit(solution)/shard_map/all_gather | solution.py:87
  482.8 2.1 copy-start.2
  485.7 133.6 %all-gather.9.cloned.1.call-start = ((), (), s32[]{:S(2)}) async-start(), calls=%async_computation.3 | async-start | bytes 2621440 | tf_op jit(solution)/shard_map/all_gather | solution.py:87
  485.8 69.3 %copy-start.5 = (f32[512,256]{1,0:T(8,128)S(1)}, f32[512,256]{1,0:T(8,128)}, u32[]{:S(2)}) copy-start(f32[512,256]{1,0:T(8,128)} %slice_divide_fusion.1) | copy-start | bytes 1572868
  575.3 62.7 %copy-start.3 = (f32[512,256]{1,0:T(8,128)S(1)}, f32[512,256]{1,0:T(8,128)}, u32[]{:S(2)}) copy-start(f32[512,256]{1,0:T(8,128)} %multiply_subtract_fusion.1) | copy-start | bytes 1572868
  575.3 108.2 %all-gather.11.cloned.1.call-start = ((), (), s32[]{:S(2)}) async-start(), calls=%async_computation.4 | async-start | bytes 2621440 | tf_op jit(solution)/shard_map/all_gather | solution.py:87
  639.4 62.6 %copy-start.4 = (f32[512,256]{1,0:T(8,128)S(1)}, f32[512,256]{1,0:T(8,128)}, u32[]{:S(2)}) copy-start(f32[512,256]{1,0:T(8,128)} %get-tuple-element.64) | copy-start | bytes 1572868
  639.5 64.5 %copy-start.1 = (bf16[256,2048]{1,0:T(8,128)(2,1)S(1)}, bf16[256,2048]{1,0:T(8,128)(2,1)}, u32[]{:S(2)}) copy-start(bf16[256,2048]{1,0:T(8,128)(2,1)} %param.11) | copy-start | bytes 3145732
Sparse Core Ops, SparseCore 0:
  36.7 316.6 reduce-scatter.1
  354.9 120.9 all-gather.12
  485.9 69.1 all-gather.6
  575.5 43.8 all-gather.8
  639.6 43.8 all-gather.10
where the time goes:
time: 711 us
  waiting for transfers between devices  572 us (80%)
  matrix products  48 us (7%)
  blocking collectives  46.1 us (6%)
  between operations  18.6 us (3%)
  other arithmetic  17.9 us (3%)
  local copies, waits for them, and re-layouts  7.23 us (1%)
    reduce_scatter x1, waiting for transfers between devices, on_device(): lax.psum_scatter(lax.dot_general(features, combined, contract_rows, preci...  317 us
    all_gather x3, waiting for transfers between devices, on_device(): lax.all_gather(residual, 'asset', axis=0, tiled=True)  152 us
    all_gather x1, waiting for transfers between devices, prefix(): gathered = jax.tree.map(lambda a: lax.all_gather(a, axis), part)  104 us
    psum x3, blocking collectives, on_device(): lax.psum((jnp.sum(residual * residual), jnp.sum(residual * image)), 'asset')  31.1 us
    dot_general x3, matrix products, on_device(): jnp.dot(system, lax.all_gather(residual, 'asset', axis=0, tiled=True), pr...  20.5 us
    dot_general x1, matrix products, on_device(): lax.dot_general(features, combined, contract_rows, precision=lax.Precisio...  19.4 us
    unnamed x2, blocking collectives  14.9 us
  transfers between devices with their start and end apart: 5, of which 5 were waited for; matrix products, arithmetic and copies ran while one was open for 1% of the time, Pallas kernels for 0%

commit v1 on v0

--- a/solution.py
+++ b/solution.py
@@ -2,10 +2,28 @@
 import jax.numpy as jnp
 from jax import lax
 from jax.sharding import PartitionSpec as P
+from jax.lax import axis_index, axis_size, ppermute
 
 ITERS = 3
 ridge_penalty = 0.05
 epsilon = 1e-06
+
+
+def draft_lanes(load, along_dim):
+    peer_axis = "asset"
+    shares = axis_size(peer_axis)
+    store = [(it, (it + 1) % shares) for it in range(shares)]
+    kept_rows = [(it, (it - 1) % shares) for it in range(shares)]
+    taken_in, work_now = ([load], [load])
+    for _ in range(shares // 2):
+        current_value = ppermute(taken_in[-1], peer_axis, store)
+        taken_in.append(current_value)
+    for _ in range((shares - 1) // 2):
+        tall = ppermute(work_now[-1], peer_axis, kept_rows)
+        work_now.append(tall)
+    low = jnp.concatenate([*taken_in[::-1], *work_now[1:]], along_dim)
+    wide_out = axis_index(peer_axis)
+    return jnp.roll(low, (wide_out - shares // 2) * load.shape[along_dim], along_dim)
 
 
 def prefix(part, axis, combine, identity):
@@ -83,9 +101,7 @@
     coef = jnp.zeros((block_size, tgt_width), jnp.float32)
     for iteration in range(ITERS):
         image = jnp.zeros((block_size, tgt_width), jnp.float32) + jnp.dot(
-            system,
-            lax.all_gather(residual, "asset", axis=0, tiled=True),
-            precision=lax.Precision.HIGHEST,
+            system, draft_lanes(residual, 0), precision=lax.Precision.HIGHEST
         )
         res_norm, res_curve = lax.psum(
             (jnp.sum(residual * residual), jnp.sum(residual * image)), "asset"

time: 711 us -> 675 us (0.949)
  the two profiles are of different devices: /device:TPU:0 before, /device:TPU:2 now
where the time goes in v1:
time: 675 us
  waiting for transfers between devices  512 us (76%)
  matrix products  52.5 us (8%)
  blocking collectives  46.1 us (7%)
  other arithmetic  23.7 us (4%)
  between operations  18.8 us (3%)
  starting transfers between devices  11.6 us (2%)
  local copies, waits for them, and re-layouts  8.43 us (1%)
    reduce_scatter x1, waiting for transfers between devices, on_device(): lax.psum_scatter(lax.dot_general(features, combined, contract_rows, preci...  315 us
    all_gather x1, waiting for transfers between devices, prefix(): gathered = jax.tree.map(lambda a: lax.all_gather(a, axis), part)  102 us
    ppermute x6, waiting for transfers between devices, draft_lanes(): current_value = ppermute(taken_in[-1], peer_axis, store)  50.1 us
    ppermute x3, waiting for transfers between devices, draft_lanes(): tall = ppermute(work_now[-1], peer_axis, kept_rows)  44.6 us
    psum x3, blocking collectives, on_device(): lax.psum((jnp.sum(residual * residual), jnp.sum(residual * image)), 'asset')  30.9 us
    dot_general x3, matrix products, on_device(): jnp.dot(system, draft_lanes(residual, 0), precision=lax.Precision.HIGHEST)  25 us
    dot_general x1, matrix products, on_device(): lax.dot_general(features, combined, contract_rows, precision=lax.Precisio...  19.4 us
    unnamed x2, blocking collectives  15.2 us
  transfers between devices with their start and end apart: 11, of which 11 were waited for; matrix products, arithmetic and copies ran while one was open for 0% of the time, Pallas kernels for 0%

profile of v1, /device:TPU:2, one launch (start us, length us, event | category | flops | bytes accessed | tf_op | source)
XLA Modules:
  0.0 674.9 jit_solution(16456075464958745450)
XLA Ops:
  9.0 8.1 %fusion.3 = f32[256,2048]{1,0:T(8,128)S(1)} fusion(bf16[256,2048]{1,0:T(8,128)(2,1)S(1)} %copy-done, f32[2048]{0:T(1024)} %param.14, f32[2048]{0:T(1024)S(1)} %add_multiply_fusion, pred[256]{0:T(512)(128)(4,1)S(1)} %iota_compare_fusion.1, bf16[1,256,256]{2,1,0:T(8,128)(2,1)} %param.10), kind=kOutput, calls=%fused_computation.31 | convolution fusion | flops 270008320 | bytes 3293440 | tf_op jit(solution)/shard_map/dot_general | solution.py:55
  17.1 19.4 %fusion.4 = f32[2048,2304]{1,0:T(8,128)} fusion(f32[256,2048]{1,0:T(8,128)S(1)} %fusion.3, f32[256,256]{1,0:T(8,128)S(1)} %convert_select_fusion), kind=kOutput, calls=%fused_computation.32 | convolution fusion | flops 14496104448 | bytes 21233664 | tf_op jit(solution)/shard_map/dot_general | solution.py:82
  36.6 315.2 %reduce-scatter.2.cloned.1.call-done = f32[512,2304]{1,0:T(8,128)} async-done(((f32[2048,2304]{1,0:T(8,128)}), f32[512,2304]{1,0:T(8,128)}) %reduce-scatter.2.cloned.1.call-update) | async-done | bytes 4718608 | tf_op jit(solution)/shard_map/reduce_scatter | solution.py:81
  353.1 9.3 %all-reduce = s32[4]{0:T(128)S(1)} all-reduce(s32[4]{0:T(128)S(1)} %bitcast_dynamic-update-slice_fusion), channel_id=3, replica_groups=mesh['grp'=2,'epoch'=4,'asset'=4] {'asset'}, use_global_device_ids=true, to_apply=%add | all-reduce | flops 4 | bytes 32
  365.0 5.9 all-reduce.1
  370.9 102.4 %all-gather.4.cloned.1.call-done = f32[2048,2304]{1,0:T(8,128)} async-done(((f32[512,2304]{1,0:T(8,128)}), f32[2048,2304]{1,0:T(8,128)}) %all-gather.4.cloned.1.call-update) | async-done | bytes 18874384 | tf_op jit(solution)/shard_map/all_gather | solution.py:31
  473.3 2.5 broadcast_in_dim.58
  475.9 15.6 %while.12 = (s32[]{:T(128)}, f32[512,2304]{1,0:T(8,128)}, f32[]{:T(128)}, s32[]{:T(128)}, f32[4,512,2304]{2,1,0:T(8,128)}, /*index=5*/f32[4]{0:T(128)S(1)}, s32[]{:T(128)}, s32[]{:T(128)}, s32[]{:T(128)}) while((s32[]{:T(128)}, f32[512,2304]{1,0:T(8,128)}, f32[]{:T(128)}, s32[]{:T(128)}, f32[4,512,2304]{2,1,0:T(8,128)}, ...), condition=%wide.region_3.4_spmd, body=%wide.region_2.3_spmd.sunk | while | flops 1179654 | bytes 14155939 | solution.py:39
  475.9 6.6 bitcast_add_fusion.2
  483.7 6.6 bitcast_add_fusion.2
  491.5 4.3 add.97
  495.9 2.1 copy-done.1
  498.0 1.7 collective-permute-start
  499.7 2.2 collective-permute-start.2
  501.9 7.3 %collective-permute-done = f32[512,256]{1,0:T(8,128)S(1)} collective-permute-done((f32[512,256]{1,0:T(8,128)S(1)}, f32[512,256]{1,0:T(8,128)S(1)}, u32[]{:S(2)}, u32[]{:S(2)}) %collective-permute-start) | collective-permute-done | bytes 524320 | tf_op jit(solution)/shard_map/ppermute | solution.py:19
  509.2 21.0 %collective-permute-done.2 = f32[512,256]{1,0:T(8,128)S(1)} collective-permute-done((f32[512,256]{1,0:T(8,128)S(1)}, f32[512,256]{1,0:T(8,128)S(1)}, u32[]{:S(2)}, u32[]{:S(2)}) %collective-permute-start.2) | collective-permute-done | bytes 524320 | tf_op jit(solution)/shard_map/ppermute | solution.py:22
  530.3 8.4 %multiply_reduce_fusion.3 = (f32[]{:T(128)}, f32[]{:T(128)}, f32[512,256]{1,0:T(8,128)S(1)}) fusion(f32[512,256]{1,0:T(8,128)S(1)} %slice_divide_fusion.1, s32[]{:T(128)S(6)} %select_n.49, f32[512,256]{1,0:T(8,128)} %collective-permute-done.1, f32[512,256]{1,0:T(8,128)S(1)} %collective-permute-done, f32[512,256]{1,0:T(8,128)S(1)} %collective-permute-done.2, ...), kind=kOutput, calls=%fused_computation.69 | convolution fusion | flops 3230662656 | bytes 7342096 | tf_op jit(solution)/shard_map/dot_general | solution.py:103
  538.6 10.5 %all-reduce.4 = (f32[]{:T(128)}, f32[]{:T(128)}) all-reduce(f32[]{:T(128)} %get-tuple-element.45, f32[]{:T(128)} %get-tuple-element.44), channel_id=1, replica_groups=mesh['grp'=2,'epoch'=4,'asset'=4] {'asset'}, use_global_device_ids=true, to_apply=%region_5.6 | all-reduce | flops 2 | bytes 16 | tf_op jit(solution)/shard_map/psum | solution.py:106
  552.0 3.4 collective-permute-start.5
  555.4 9.0 %collective-permute-done.3 = f32[512,256]{1,0:T(8,128)S(1)} collective-permute-done((f32[512,256]{1,0:T(8,128)S(1)}, f32[512,256]{1,0:T(8,128)S(1)}, u32[]{:S(2)}, u32[]{:S(2)}) %collective-permute-start.3) | collective-permute-done | bytes 524320 | tf_op jit(solution)/shard_map/ppermute | solution.py:19
  564.4 13.1 %collective-permute-done.5 = f32[512,256]{1,0:T(8,128)S(1)} collective-permute-done((f32[512,256]{1,0:T(8,128)S(1)}, f32[512,256]{1,0:T(8,128)S(1)}, u32[]{:S(2)}, u32[]{:S(2)}) %collective-permute-start.5) | collective-permute-done | bytes 524320 | tf_op jit(solution)/shard_map/ppermute | solution.py:22
  577.5 9.3 %collective-permute-done.4 = f32[512,256]{1,0:T(8,128)S(1)} collective-permute-done((f32[512,256]{1,0:T(8,128)S(1)}, f32[512,256]{1,0:T(8,128)S(1)}, u32[]{:S(2)}, u32[]{:S(2)}) %collective-permute-start.4) | collective-permute-done | bytes 524320 | tf_op jit(solution)/shard_map/ppermute | solution.py:19
  586.8 8.3 %multiply_reduce_fusion.1 = (f32[]{:T(128)}, f32[]{:T(128)}, f32[512,256]{1,0:T(8,128)S(1)}) fusion(f32[512,256]{1,0:T(8,128)S(1)} %multiply_subtract_fusion.1, s32[]{:T(128)S(6)} %select_n.49, f32[512,256]{1,0:T(8,128)S(1)} %collective-permute-done.4, f32[512,256]{1,0:T(8,128)S(1)} %collective-permute-done.3, f32[512,256]{1,0:T(8,128)S(1)} %collective-permute-done.5, ...), kind=kOutput, calls=%fused_computation.66 | convolution fusion | flops 3230662656 | bytes 7342096 | tf_op jit(solution)/shard_map/dot_general | solution.py:103
  595.2 9.7 %all-reduce.3 = (f32[]{:T(128)}, f32[]{:T(128)}) all-reduce(f32[]{:T(128)} %get-tuple-element.43, f32[]{:T(128)} %get-tuple-element.42), channel_id=1, replica_groups=mesh['grp'=2,'epoch'=4,'asset'=4] {'asset'}, use_global_device_ids=true, to_apply=%region_9.11 | all-reduce | flops 2 | bytes 16 | tf_op jit(solution)/shard_map/psum | solution.py:106
  606.9 1.3 collective-permute-start.6
  608.2 2.5 collective-permute-start.8
  610.7 12.5 %collective-permute-done.6 = f32[512,256]{1,0:T(8,128)S(1)} collective-permute-done((f32[512,256]{1,0:T(8,128)S(1)}, f32[512,256]{1,0:T(8,128)S(1)}, u32[]{:S(2)}, u32[]{:S(2)}) %collective-permute-start.6) | collective-permute-done | bytes 524320 | tf_op jit(solution)/shard_map/ppermute | solution.py:19
  623.3 10.5 %collective-permute-done.8 = f32[512,256]{1,0:T(8,128)S(1)} collective-permute-done((f32[512,256]{1,0:T(8,128)S(1)}, f32[512,256]{1,0:T(8,128)S(1)}, u32[]{:S(2)}, u32[]{:S(2)}) %collective-permute-start.8) | collective-permute-done | bytes 524320 | tf_op jit(solution)/shard_map/ppermute | solution.py:22
  633.8 11.9 %collective-permute-done.7 = f32[512,256]{1,0:T(8,128)} collective-permute-done((f32[512,256]{1,0:T(8,128)S(1)}, f32[512,256]{1,0:T(8,128)}, u32[]{:S(2)}, u32[]{:S(2)}) %collective-permute-start.7) | collective-permute-done | bytes 524320 | tf_op jit(solution)/shard_map/ppermute | solution.py:19
  645.7 8.3 %fusion.41 = f32[]{:T(128)} fusion(f32[512,256]{1,0:T(8,128)S(1)} %get-tuple-element.65, s32[]{:T(128)S(6)} %select_n.49, f32[512,256]{1,0:T(8,128)} %collective-permute-done.7, f32[512,256]{1,0:T(8,128)S(1)} %collective-permute-done.6, f32[512,256]{1,0:T(8,128)S(1)} %collective-permute-done.8, f32[512,2304]{1,0:T(8,128)} %copy-done.1, ...), kind=kOutput, calls=%fused_computation.61 | convolution fusion | flops 3230400512 | bytes 6817804 | tf_op jit(solution)/shard_map/dot_general | solution.py:103
  654.1 10.7 %all-reduce.2 = (f32[]{:T(128)}, f32[]{:T(128)}) all-reduce(f32[]{:T(128)} %get-tuple-element.64, f32[]{:T(128)} %fusion.41), channel_id=1, replica_groups=mesh['grp'=2,'epoch'=4,'asset'=4] {'asset'}, use_global_device_ids=true, to_apply=%region_13.15 | all-reduce | flops 2 | bytes 16 | tf_op jit(solution)/shard_map/psum | solution.py:106
  666.0 2.0 multiply_bitcast_fusion
  (32 shorter events, 8.8 us)
Async XLA Ops:
  6.5 2.5 copy-start
  6.5 345.3 %reduce-scatter.2.cloned.1.call-start = ((), (), s32[]{:S(2)}) async-start(), calls=%async_computation.1 | async-start | bytes 23592960 | tf_op jit(solution)/shard_map/reduce_scatter | solution.py:81
  36.5 315.3 %copy-start.3 = (u32[32]{0:T(128)S(1)}, u32[32]{0:T(128)}, u32[]{:S(2)}) copy-start(u32[32]{0:T(128)} %constant.79) | copy-start | bytes 388
  36.6 327.1 %copy-start.2 = (u32[32]{0:T(128)S(1)}, u32[32]{0:T(128)}, u32[]{:S(2)}) copy-start(u32[32]{0:T(128)} %constant.84) | copy-start | bytes 388
  36.6 436.8 %all-gather.4.cloned.1.call-start = ((), (), s32[]{:S(2)}) async-start(), calls=%async_computation.2 | async-start | bytes 23592960 | tf_op jit(solution)/shard_map/all_gather | solution.py:31
  495.8 2.1 copy-start.1
  498.0 11.1 %collective-permute-start = (f32[512,256]{1,0:T(8,128)S(1)}, f32[512,256]{1,0:T(8,128)S(1)}, u32[]{:S(2)}, u32[]{:S(2)}) collective-permute-start(f32[512,256]{1,0:T(8,128)S(1)} %slice_divide_fusion.1), channel_id=1, source_target_pairs={{0,1},{1,2},{2,3},{3,0},{4,5},{5,6},{6,7},{7,4},{8,9},{9,10},{10,1... | collective-permute-start | bytes 1572872 | tf_op jit(solution)/shard_map/ppermute | solution.py:19
  499.7 30.4 %collective-permute-start.2 = (f32[512,256]{1,0:T(8,128)S(1)}, f32[512,256]{1,0:T(8,128)S(1)}, u32[]{:S(2)}, u32[]{:S(2)}) collective-permute-start(f32[512,256]{1,0:T(8,128)S(1)} %slice_divide_fusion.1), channel_id=1, source_target_pairs={{0,3},{1,0},{2,1},{3,2},{4,7},{5,4},{6,5},{7,6},{8,11},{9,8},{10,9... | collective-permute-start | bytes 1572872 | tf_op jit(solution)/shard_map/ppermute | solution.py:22
  509.1 21.1 %collective-permute-start.1 = (f32[512,256]{1,0:T(8,128)S(1)}, f32[512,256]{1,0:T(8,128)}, u32[]{:S(2)}, u32[]{:S(2)}) collective-permute-start(f32[512,256]{1,0:T(8,128)S(1)} %collective-permute-done), channel_id=1, source_target_pairs={{0,1},{1,2},{2,3},{3,0},{4,5},{5,6},{6,7},{7,4},{8,9},{9,10},{10,1... | collective-permute-start | bytes 1572872 | tf_op jit(solution)/shard_map/ppermute | solution.py:19
  551.5 12.9 %collective-permute-start.3 = (f32[512,256]{1,0:T(8,128)S(1)}, f32[512,256]{1,0:T(8,128)S(1)}, u32[]{:S(2)}, u32[]{:S(2)}) collective-permute-start(f32[512,256]{1,0:T(8,128)S(1)} %multiply_subtract_fusion.1), channel_id=1, source_target_pairs={{0,1},{1,2},{2,3},{3,0},{4,5},{5,6},{6,7},{7,4},{8,9},{9,10},{10,1... | collective-permute-start | bytes 1572872 | tf_op jit(solution)/shard_map/ppermute | solution.py:19
  552.0 25.5 %collective-permute-start.5 = (f32[512,256]{1,0:T(8,128)S(1)}, f32[512,256]{1,0:T(8,128)S(1)}, u32[]{:S(2)}, u32[]{:S(2)}) collective-permute-start(f32[512,256]{1,0:T(8,128)S(1)} %multiply_subtract_fusion.1), channel_id=1, source_target_pairs={{0,3},{1,0},{2,1},{3,2},{4,7},{5,4},{6,5},{7,6},{8,11},{9,8},{10,9... | collective-permute-start | bytes 1572872 | tf_op jit(solution)/shard_map/ppermute | solution.py:22
  564.4 22.4 %collective-permute-start.4 = (f32[512,256]{1,0:T(8,128)S(1)}, f32[512,256]{1,0:T(8,128)S(1)}, u32[]{:S(2)}, u32[]{:S(2)}) collective-permute-start(f32[512,256]{1,0:T(8,128)S(1)} %collective-permute-done.3), channel_id=1, source_target_pairs={{0,1},{1,2},{2,3},{3,0},{4,5},{5,6},{6,7},{7,4},{8,9},{9,10},{10,1... | collective-permute-start | bytes 1572872 | tf_op jit(solution)/shard_map/ppermute | solution.py:19
  606.9 16.3 %collective-permute-start.6 = (f32[512,256]{1,0:T(8,128)S(1)}, f32[512,256]{1,0:T(8,128)S(1)}, u32[]{:S(2)}, u32[]{:S(2)}) collective-permute-start(f32[512,256]{1,0:T(8,128)S(1)} %get-tuple-element.65), channel_id=1, source_target_pairs={{0,1},{1,2},{2,3},{3,0},{4,5},{5,6},{6,7},{7,4},{8,9},{9,10},{10,1... | collective-permute-start | bytes 1572872 | tf_op jit(solution)/shard_map/ppermute | solution.py:19
  608.2 25.6 %collective-permute-start.8 = (f32[512,256]{1,0:T(8,128)S(1)}, f32[512,256]{1,0:T(8,128)S(1)}, u32[]{:S(2)}, u32[]{:S(2)}) collective-permute-start(f32[512,256]{1,0:T(8,128)S(1)} %get-tuple-element.65), channel_id=1, source_target_pairs={{0,3},{1,0},{2,1},{3,2},{4,7},{5,4},{6,5},{7,6},{8,11},{9,8},{10,9... | collective-permute-start | bytes 1572872 | tf_op jit(solution)/shard_map/ppermute | solution.py:22
  623.2 22.5 %collective-permute-start.7 = (f32[512,256]{1,0:T(8,128)S(1)}, f32[512,256]{1,0:T(8,128)}, u32[]{:S(2)}, u32[]{:S(2)}) collective-permute-start(f32[512,256]{1,0:T(8,128)S(1)} %collective-permute-done.6), channel_id=1, source_target_pairs={{0,1},{1,2},{2,3},{3,0},{4,5},{5,6},{6,7},{7,4},{8,9},{9,10},{10,1... | collective-permute-start | bytes 1572872 | tf_op jit(solution)/shard_map/ppermute | solution.py:19
Sparse Core Ops, SparseCore 0:
  36.7 315.1 reduce-scatter.1
  353.4 119.8 all-gather.3
